TPU v7x, 32 devices: a whole 2x2x4 slice. The times are simulated.
32 devices in a mesh: stream: 8 (over y, x, core), tp: 4 (over z).
Axes of the slice: x: 2, y: 2, z: 4, core: 2. Of those that a mesh axis runs over, the one named last changes fastest.
Arguments:
- tokens: bfloat16 [12288, 3072], P('stream', 'tp'), may hold values from -6 to 6
- qkv_weight: bfloat16 [3072, 3, 2048], P('stream', None, 'tp'), may hold values from -0.109375 to 0.109375
- gate_weight: bfloat16 [3072, 2048], P('stream', 'tp'), may hold values from -0.109375 to 0.109375
- out_weight: bfloat16 [2048, 3072], P('tp', 'stream'), may hold values from -0.125 to 0.125
- log_decay: float32 [32, 12288], P('tp', 'stream'), may hold values from -1 to 0
- states: float32 [96, 32, 64, 64], P('stream', 'tp'), may hold values from -48 to 48
- dest_slot: int32 [96], P('stream'), may hold values from 0 to 95, as said below
- valid: int32 [96], P('stream'), may hold values from 1 to 128
Outputs:
- mixed: bfloat16 [12288, 3072], P('stream', 'tp')
- new_states: float32 [96, 32, 64, 64], P('stream', 'tp')
Inputs may be any that keep to these rules, and one draw needn't show every extreme that they name: dest_slot is a permutation of the streams; of the 12 streams of one device, at most 2 have new positions on any one device, and that many do for some pair of devices.
All inputs are finite; a program needn't handle non-finite values.
Results may differ from a plain program's by a relative error of at most 0.0058.
Values may be sent and summed in bfloat16 or wider, within the bound.
A program may use at most 128 MiB of HBM per device.

v0:
```python
import functools

import jax
import jax.numpy as jnp
from jax import lax
from jax.experimental import pallas as pl
from jax.experimental.pallas import tpu as pltpu
from jax.sharding import PartitionSpec as P

HD = 64
WINDOW_LENGTH = 128
CHUNKS = 2


def move_states(states, dest_slot):
    streams = states.shape[0]
    node_count = lax.axis_size("stream")
    capacity = (streams + node_count - 1) // node_count
    target = dest_slot // streams
    places = dest_slot % streams
    order = jnp.arange(streams, dtype=jnp.int32)
    earlier = (target[None, :] == target[:, None]) & (order[None, :] < order[:, None])
    ranking = jnp.sum(earlier.astype(jnp.int32), axis=1)
    position = target * capacity + ranking
    tail_shape = states.shape[1:]
    outgoing = (
        jnp.zeros((node_count * capacity,) + tail_shape, jnp.float32).at[position].set(states)
    )
    outgoing = outgoing.reshape((node_count, capacity) + tail_shape)
    labels = jnp.full((node_count * capacity,), streams, jnp.int32).at[position].set(places)
    labels = labels.reshape(node_count, capacity)
    incoming, incoming_labels = (
        lax.all_to_all(outgoing, "stream", split_axis=0, concat_axis=0, tiled=True),
        lax.all_to_all(labels, "stream", split_axis=0, concat_axis=0, tiled=True),
    )
    flat_states = incoming.reshape((node_count * capacity,) + tail_shape)
    flat_labels = incoming_labels.reshape(node_count * capacity)
    placed = jnp.zeros((streams + 1,) + tail_shape, jnp.float32).at[flat_labels].set(flat_states)
    return placed[:streams]


MESH = pl.DeviceIdType.MESH


def greet(targets):
    barrier = pltpu.get_barrier_semaphore()
    for target in targets:
        pl.semaphore_signal(barrier, inc=1, device_id=target, device_id_type=MESH)
    pl.semaphore_wait(barrier, len(targets))


def remote(src, dst, send, recv, target):
    return pltpu.make_async_remote_copy(
        src_ref=src, dst_ref=dst, send_sem=send, recv_sem=recv, device_id=target, device_id_type=MESH
    )


def gather_kernel(chips, planes, w_ref, o_ref, out_ref, col_ref, send1, recv1, send2, recv2, sendz, recvz, local):
    me = lax.axis_index("stream")
    tp = lax.axis_index("tp")
    chip, core = me // 2, me % 2
    per = chips * 2 // planes
    owner = me // per
    mine = owner == tp
    sibling = (chip * 2 + (1 - core), tp)
    peers = [(((chip + d) % chips) * 2 + core, tp) for d in range(1, chips)]
    column = [(me, (tp + d) % planes) for d in range(1, planes)]
    greet(peers + [sibling] + column)
    sends = []
    for d in range(1, chips):
        copy = remote(w_ref, out_ref.at[me], send1.at[d], recv1.at[d], peers[d - 1])
        copy.start()
        sends.append(copy)
    copy = remote(w_ref, out_ref.at[me], send2.at[0], recv2.at[0], sibling)
    copy.start()
    sends.append(copy)
    hop = remote(o_ref, col_ref.at[tp], sendz, recvz.at[tp], (me, owner))

    @pl.when(jnp.logical_not(mine))
    def _():
        hop.start()

    own = pltpu.make_async_copy(w_ref, out_ref.at[me], local.at[0])
    own.start()
    kept = pltpu.make_async_copy(o_ref, col_ref.at[tp], local.at[1])
    kept.start()
    for d in range(1, chips):
        source = ((chip - d + chips) % chips) * 2 + core
        slot = out_ref.at[source]
        remote(w_ref, slot, send1.at[d], recv1.at[d], peers[d - 1]).wait_recv()
        copy = remote(slot, slot, send2.at[d], recv2.at[d], sibling)
        copy.start()
        sends.append(copy)
    for d in range(chips):
        source = ((chip - d + chips) % chips) * 2 + (1 - core)
        remote(w_ref, out_ref.at[source], send2.at[d], recv2.at[d], sibling).wait_recv()

    @pl.when(mine)
    def _():
        for d in range(1, planes):
            source = (tp + d) % planes
            remote(o_ref, col_ref.at[source], sendz, recvz.at[source], (me, source)).wait_recv()

    @pl.when(jnp.logical_not(mine))
    def _():
        hop.wait_send()

    for copy in sends:
        copy.wait_send()
    own.wait()
    kept.wait()


def gather_rows(weight, out_weight):
    count, planes = lax.axis_size("stream"), lax.axis_size("tp")
    chips = count // 2
    dma = pltpu.SemaphoreType.DMA
    anywhere = pl.BlockSpec(memory_space=pl.ANY)
    return pl.pallas_call(
        functools.partial(gather_kernel, chips, planes),
        out_shape=(
            jax.ShapeDtypeStruct((count,) + weight.shape, weight.dtype),
            jax.ShapeDtypeStruct((planes,) + out_weight.shape, out_weight.dtype),
        ),
        in_specs=[anywhere, anywhere],
        out_specs=(anywhere, anywhere),
        scratch_shapes=[dma((chips,))] * 4 + [dma, dma((planes,)), dma((2,))],
        compiler_params=pltpu.CompilerParams(collective_id=0, has_side_effects=True),
        cost_estimate=pl.CostEstimate(flops=0, bytes_accessed=200_000_000, transcendentals=0),
        name="gather_rows",
    )(weight, out_weight)


def spread_kernel(count, planes, col_ref, out_ref, sendx, recvx, sends, recvs, local):
    me = lax.axis_index("stream")
    tp = lax.axis_index("tp")
    chips, per = count // 2, count // planes
    chip, core = me // 2, me % 2
    sibling = (chip * 2 + (1 - core), tp)
    peers = [(((chip + d) % chips) * 2 + core, tp) for d in range(1, chips)]
    greet(peers + [sibling])
    owner, place = me // per, me % per
    mine = owner == tp

    @pl.when(mine)
    def _():
        for d in range(1, chips):
            remote(col_ref, out_ref.at[place], sendx.at[d], recvx.at[place // 2], peers[d - 1]).start()
        own = pltpu.make_async_copy(col_ref, out_ref.at[place], local)
        own.start()
        own.wait()

    for i in range(per // 2):
        slot = out_ref.at[2 * i + core]
        source = tp * per + 2 * i + core

        @pl.when(source != me)
        def _():
            remote(slot, slot, sendx.at[0], recvx.at[i], sibling).wait_recv()

        remote(slot, slot, sends.at[i], recvs.at[i], sibling).start()
    for i in range(per // 2):
        other = out_ref.at[2 * i + (1 - core)]
        remote(other, other, sends.at[i], recvs.at[i], sibling).wait_recv()
    for i in range(per // 2):
        slot = out_ref.at[2 * i + core]
        remote(slot, slot, sends.at[i], recvs.at[i], sibling).wait_send()

    @pl.when(mine)
    def _():
        for d in range(1, chips):
            remote(col_ref, out_ref.at[place], sendx.at[d], recvx.at[place // 2], peers[d - 1]).wait_send()


def spread_columns(columns):
    count, planes = lax.axis_size("stream"), lax.axis_size("tp")
    chips, per = count // 2, count // planes
    dma = pltpu.SemaphoreType.DMA
    return pl.pallas_call(
        functools.partial(spread_kernel, count, planes),
        out_shape=jax.ShapeDtypeStruct((per,) + columns.shape, columns.dtype),
        in_specs=[pl.BlockSpec(memory_space=pl.ANY)],
        out_specs=pl.BlockSpec(memory_space=pl.ANY),
        scratch_shapes=[dma((chips,)), dma((per // 2,)), dma((per // 2,)), dma((per // 2,)), dma],
        compiler_params=pltpu.CompilerParams(collective_id=1, has_side_effects=True),
        cost_estimate=pl.CostEstimate(flops=0, bytes_accessed=200_000_000, transcendentals=0),
        name="spread_columns",
    )(columns)


def halves(x):
    high = x.astype(jnp.bfloat16)
    return high, (x - high.astype(jnp.float32)).astype(jnp.bfloat16)


def product(a, b, left, right):
    return lax.dot_general(a, b, (((left,), (right,)), ((), ())), preferred_element_type=jnp.float32)


def attend_kernel(first, heads, valid_ref, proj_ref, decay_ref, moved_ref, *refs):
    hidden_ref, updated_ref = refs[-2:]
    length, width = WINDOW_LENGTH, heads * HD
    count = valid_ref[first + pl.program_id(0)]
    column = lax.broadcasted_iota(jnp.int32, (length, 1), 0)
    live = (column < count).astype(jnp.float32)
    rows = lax.broadcasted_iota(jnp.int32, (length, length), 0)
    cols = lax.broadcasted_iota(jnp.int32, (length, length), 1)
    live_row = lax.broadcasted_iota(jnp.int32, (heads, length), 1) < count
    decay = jnp.where(live_row, decay_ref[...], 0.0)
    ones = (rows <= cols).astype(jnp.float32)
    across = lax.dot_general(
        decay,
        ones,
        (((1,), (0,)), ((), ())),
        precision=lax.Precision.HIGHEST,
        preferred_element_type=jnp.float32,
    )
    down = across.T
    causal = rows >= cols
    for pair in range(heads // 2):
        block = slice(pair * 2 * HD, (pair + 1) * 2 * HD)

        def active(part):
            x = proj_ref[:, part * width + block.start : part * width + block.stop]
            return x * jax.nn.sigmoid(x)

        queries = active(0).astype(jnp.bfloat16)
        keys = (active(1) * live).astype(jnp.bfloat16)
        values = (active(2) * live).astype(jnp.bfloat16)
        gates = jax.nn.sigmoid(proj_ref[:, 3 * width + block.start : 3 * width + block.stop]) * live
        outs = []
        for side in range(2):
            h = 2 * pair + side
            lanes = slice(side * HD, (side + 1) * HD)
            q, k, v = queries[:, lanes], keys[:, lanes], values[:, lanes]
            along, above = down[:, h : h + 1], across[h : h + 1, :]
            last = across[h : h + 1, length - 1 :]
            weights = jnp.where(causal, jnp.exp(jnp.minimum(along - above, 0.0)), 0.0)
            probs = (product(q, k, 1, 1) * weights).astype(jnp.bfloat16)
            old = moved_ref[0, h]
            high, low = halves(old)
            carried = product(q, high, 1, 0) + product(q, low, 1, 0)
            attended = product(probs, v, 1, 0) + carried * jnp.exp(along)
            high, low = halves(k.astype(jnp.float32) * jnp.exp(last - along))
            updated_ref[0, h] = jnp.exp(last) * old + (product(high, v, 0, 0) + product(low, v, 0, 0))
            mean_square = jnp.mean(attended * attended, axis=1, keepdims=True)
            outs.append(attended * lax.rsqrt(mean_square + 1e-05))
        hidden_ref[:, block] = (jnp.concatenate(outs, axis=1) * gates).astype(jnp.bfloat16)


def attend(projected, valid, log_decay, moved, first, part, earlier):
    streams, heads = moved.shape[:2]
    length, width = WINDOW_LENGTH, heads * HD
    in_specs = [
        pl.BlockSpec((length, 4 * width), lambda i, v: (i, 0)),
        pl.BlockSpec((heads, length), lambda i, v: (0, first + i)),
        pl.BlockSpec((1, heads, HD, HD), lambda i, v: (first + i, 0, 0, 0)),
    ]
    operands = [projected, log_decay, moved]
    aliases = {}
    if earlier is not None:
        in_specs.append(pl.BlockSpec(memory_space=pl.ANY))
        operands.append(earlier)
        aliases = {4: 1}
    return pl.pallas_call(
        functools.partial(attend_kernel, first, heads),
        out_shape=(
            jax.ShapeDtypeStruct((part * length, width), jnp.bfloat16),
            jax.ShapeDtypeStruct(moved.shape, jnp.float32),
        ),
        grid_spec=pltpu.PrefetchScalarGridSpec(
            num_scalar_prefetch=1,
            grid=(part,),
            in_specs=in_specs,
            out_specs=(
                pl.BlockSpec((length, width), lambda i, v: (i, 0)),
                pl.BlockSpec((1, heads, HD, HD), lambda i, v: (first + i, 0, 0, 0)),
            ),
        ),
        input_output_aliases=aliases,
        cost_estimate=pl.CostEstimate(flops=0, bytes_accessed=40_000_000, transcendentals=0),
        name="attend",
    )(valid, *operands)


def body(tokens, qkv_weight, gate_weight, out_weight, log_decay, states, dest_slot, valid):
    streams, heads = states.shape[:2]
    width = heads * HD
    chunks = CHUNKS if streams % CHUNKS == 0 else 1
    part = streams // chunks
    rows = part * WINDOW_LENGTH
    features = [
        lax.all_gather(tokens[c * rows : (c + 1) * rows], "tp", axis=1, tiled=True)
        for c in range(chunks)
    ]
    local = jnp.concatenate([qkv_weight.reshape(-1, 3 * width), gate_weight], axis=1)
    moved = move_states(states, dest_slot)
    weights, columns = gather_rows(local, out_weight)
    weights = weights.reshape(-1, 4 * width)
    gathered, updated = [], None
    for c in range(chunks):
        projected = jnp.dot(features[c], weights, preferred_element_type=jnp.float32)
        hidden, updated = attend(projected, valid, log_decay, moved, c * part, part, updated)
        gathered.append(lax.all_gather(hidden, "tp", axis=1, tiled=True))
    columns, _ = lax.optimization_barrier((columns, hidden))
    spread = spread_columns(columns)
    per = spread.shape[0]
    full_rows = spread.reshape(per, -1, out_weight.shape[1]).transpose(1, 0, 2)
    full_rows = full_rows.reshape(full_rows.shape[0], -1)
    mixed = [
        jnp.dot(part_heads, full_rows, preferred_element_type=jnp.float32).astype(jnp.bfloat16)
        for part_heads in gathered
    ]
    return (jnp.concatenate(mixed, axis=0), updated)


def solution(mesh):
    return jax.shard_map(
        body,
        mesh=mesh,
        in_specs=(
            P("stream", "tp"),
            P("stream", None, "tp"),
            P("stream", "tp"),
            P("tp", "stream"),
            P("tp", "stream"),
            P("stream", "tp", None, None),
            P("stream"),
            P("stream"),
        ),
        out_specs=(P("stream", "tp"), P("stream", "tp", None, None)),
        check_vma=False,
    )
```

profile of v0, /device:TPU:0, one launch (start us, length us, event | category | flops | bytes accessed | tf_op | source)
XLA Modules:
  0.0 390.0 jit_solution(4936469074136130817)
XLA Ops:
  7.2 3.2 fusion.4
  10.5 0.7 all-gather.9.cloned.1.call-update
  11.5 0.6 scatter_custom_fusion
  12.1 0.7 all_to_all.9
  12.8 5.2 %all-to-all-start = ((s32[8,1,2]{2,1,0:T(1,128)}), s32[8,1,2]{2,1,0:T(1,128)S(1)}, u32[]{:S(2)}, u32[]{:S(2)}) async-start(s32[8,1,2]{2,1,0:T(1,128)} %bitcast.3), calls=%async_computation | async-start | bytes 8192 | tf_op jit(solution)/shard_map/all_to_all | solution.py:34
  17.9 2.5 broadcast_in_dim.8
  20.4 6.4 %scatter_fusion = f32[16,8,64,64]{3,2,1,0:T(8,128)} fusion(f32[16,8,64,64]{3,2,1,0:T(8,128)} %broadcast_in_dim.8, s32[12]{0:T(128)S(1)} %compare_select_fusion.1, f32[12,8,64,64]{3,2,1,0:T(8,128)S(1)} %copy-done.1), kind=kCustom, calls=%fused_computation.1 | custom fusion | bytes 4718640 | tf_op jit(solution)/shard_map/scatter | solution.py:27
  26.8 7.2 %reshape.104 = f32[8,1,65536]{2,1,0:T(1,128)} reshape(f32[8,2,8,64,64]{4,3,2,1,0:T(8,128)} %bitcast.23) | data formatting | bytes 4194304
  34.0 4.3 %all-to-all-start.1 = ((f32[8,1,65536]{2,1,0:T(1,128)}), f32[8,1,65536]{2,1,0:T(1,128)S(1)}, u32[]{:S(2)}, u32[]{:S(2)}) async-start(f32[8,1,65536]{2,1,0:T(1,128)} %reshape.104), calls=%async_computation.1 | async-start | bytes 4194304 | tf_op jit(solution)/shard_map/all_to_all | solution.py:33
  38.3 1.4 copy.25
  39.7 1.6 copy.26
  41.3 2.4 pad_maximum_fusion.1.w_ref
  43.6 93.7 %gather_rows.1 = (bf16[8,384,2048]{2,1,0:T(8,128)(2,1)}, bf16[4,512,384]{2,1,0:T(8,128)(2,1)}) custom-call(bf16[384,2048]{1,0:T(8,128)(2,1)} %pad_maximum_fusion.1.w_ref, bf16[512,384]{1,0:T(8,128)(2,1)} %o_ref.1), custom_call_target="tpu_custom_call" | custom-call | bytes 200000000 | tf_op jit(solution)/shard_map/gather_rows/pallas_call | solution.py:119
  137.3 0.5 broadcast.53
  137.8 0.7 reduce.3
  138.6 1.3 copy-done
  140.4 7.2 %reduce.4 = f32[8,65536]{1,0:T(8,128)S(1)} reduce(f32[8,1,65536]{2,1,0:T(1,128)} %copy-done, f32[]{:T(128)} %broadcast.54), dimensions={1}, to_apply=%all_to_all.11.reduce_sub_computation | reduce | bytes 4194308 | tf_op jit(solution)/shard_map/all_to_all | solution.py:33
  147.6 3.6 reshape.105
  151.6 4.4 %scatter_fusion.1 = f32[13,8,64,64]{3,2,1,0:T(8,128)S(1)} fusion(f32[13,8,64,64]{3,2,1,0:T(8,128)S(1)} %broadcast_in_dim.6, s32[16]{0:T(128)S(1)} %fusion.1, f32[16,8,64,64]{3,2,1,0:T(8,128)} %bitcast.24), kind=kCustom, calls=%fused_computation.2 | custom fusion | bytes 6291520 | tf_op jit(solution)/shard_map/scatter | solution.py:38
  156.1 1.9 slice.12.moved_ref
  158.0 15.9 %convolution_bitcast_fusion.1.proj_ref = f32[768,2048]{1,0:T(8,128)} fusion(bf16[768,3072]{1,0:T(8,128)(2,1)} %all-gather.5.cloned.1.call-done, bf16[3072,2048]{1,0:T(8,128)(2,1)} %bitcast.29), kind=kOutput, calls=%fused_computation.4 | convolution fusion | flops 9663676416 | bytes 23592960 | tf_op jit(solution)/shard_map/dot_general | solution.py:302
  174.0 18.7 %attend.2 = (bf16[768,512]{1,0:T(8,128)(2,1)}, f32[12,8,64,64]{3,2,1,0:T(8,128)}) custom-call(s32[12]{0:T(128)} %valid_ref.3, f32[768,2048]{1,0:T(8,128)} %convolution_bitcast_fusion.1.proj_ref, f32[8,1536]{1,0:T(8,128)} %decay_ref.3, f32[12,8,64,64]{3,2,1,0:T(8,128)} %slice.12.moved_ref), custom_call_target="tpu_custom_call" | custom-call | bytes 40000000 | tf_op jit(solution)/shard_map/attend/pallas_call | solution.py:265
  192.7 24.2 %all-gather.9.cloned.1.call-done = bf16[768,3072]{1,0:T(8,128)(2,1)} async-done(((bf16[768,768]{1,0:T(8,128)(2,1)}), bf16[768,3072]{1,0:T(8,128)(2,1)}) %all-gather.9.cloned.1.call-update) | async-done | bytes 4718608 | tf_op jit(solution)/shard_map/all_gather | solution.py:293
  216.9 15.9 %convolution_bitcast_fusion.proj_ref = f32[768,2048]{1,0:T(8,128)} fusion(bf16[768,3072]{1,0:T(8,128)(2,1)} %all-gather.9.cloned.1.call-done, bf16[3072,2048]{1,0:T(8,128)(2,1)} %bitcast.30), kind=kOutput, calls=%fused_computation.3 | convolution fusion | flops 9663676416 | bytes 23592960 | tf_op jit(solution)/shard_map/dot_general | solution.py:302
  232.8 18.8 %attend.3 = (bf16[768,512]{1,0:T(8,128)(2,1)}, f32[12,8,64,64]{3,2,1,0:T(8,128)}) custom-call(s32[12]{0:T(128)} %valid_ref.3, f32[768,2048]{1,0:T(8,128)} %convolution_bitcast_fusion.proj_ref, f32[8,1536]{1,0:T(8,128)} %decay_ref.3, f32[12,8,64,64]{3,2,1,0:T(8,128)} %slice.12.moved_ref, ...), custom_call_target="tpu_custom_call", output_to_operand_aliasing={{1}: (4, {})} | custom-call | bytes 40000000 | tf_op jit(solution)/shard_map/attend/pallas_call | solution.py:265
  251.7 0.5 all-gather.7.cloned.1.call-update
  252.2 70.3 %spread_columns.1 = bf16[2,4,512,384]{3,2,1,0:T(8,128)(2,1)} custom-call(bf16[4,512,384]{2,1,0:T(8,128)(2,1)} %get-tuple-element.14.col_ref), custom_call_target="tpu_custom_call" | custom-call | bytes 200000000 | tf_op jit(solution)/shard_map/spread_columns/pallas_call | solution.py:179
  322.5 3.5 copy.30
  326.0 5.5 %convolution_convert_fusion = bf16[768,768]{1,0:T(8,128)(2,1)} fusion(bf16[768,2048]{1,0:T(8,128)(2,1)} %all-gather.11.cloned.1.call-done, bf16[2048,768]{0,1:T(8,128)(2,1)S(1)} %bitcast.27), kind=kOutput, calls=%fused_computation.7 | convolution fusion | flops 2416508928 | bytes 7471104 | tf_op jit(solution)/shard_map/dot_general | solution.py:311
  331.5 45.7 %all-gather.7.cloned.1.call-done = bf16[768,2048]{1,0:T(8,128)(2,1)} async-done(((bf16[768,512]{1,0:T(8,128)(2,1)}), bf16[768,2048]{1,0:T(8,128)(2,1)}) %all-gather.7.cloned.1.call-update) | async-done | bytes 3145744 | tf_op jit(solution)/shard_map/all_gather | solution.py:304
  377.3 4.6 %convolution_convert_fusion.1 = bf16[768,768]{1,0:T(8,128)(2,1)S(1)} fusion(bf16[768,2048]{1,0:T(8,128)(2,1)} %all-gather.7.cloned.1.call-done, bf16[2048,768]{0,1:T(8,128)(2,1)S(1)} %bitcast.28), kind=kOutput, calls=%fused_computation.8 | convolution fusion | flops 2416508928 | bytes 7471104 | tf_op jit(solution)/shard_map/dot_general | solution.py:311
  381.9 1.6 pad_maximum_fusion
  (26 shorter events, 1.4 us)
Async XLA Ops:
  7.2 4.1 %copy-start.4 = (s32[12]{0:T(128)S(1)}, s32[12]{0:T(128)}, u32[]{:S(2)}) copy-start(s32[12]{0:T(128)} %param.14) | copy-start | bytes 148
  7.2 150.9 %all-gather.5.cloned.1.call-start = ((), (), s32[]{:S(2)}) async-start(), calls=%async_computation.2 | async-start | bytes 5898240 | tf_op jit(solution)/shard_map/all_gather | solution.py:293
  10.5 9.9 %copy-start.1 = (f32[12,8,64,64]{3,2,1,0:T(8,128)S(1)}, f32[12,8,64,64]{3,2,1,0:T(8,128)}, u32[]{:S(2)}) copy-start(f32[12,8,64,64]{3,2,1,0:T(8,128)} %param.13) | copy-start | bytes 4718596
  10.5 206.4 %all-gather.9.cloned.1.call-start = ((), (), s32[]{:S(2)}) async-start(), calls=%async_computation.4 | async-start | bytes 5898240 | tf_op jit(solution)/shard_map/all_gather | solution.py:293
  12.8 21.2 %all-to-all-start = ((s32[8,1,2]{2,1,0:T(1,128)}), s32[8,1,2]{2,1,0:T(1,128)S(1)}, u32[]{:S(2)}, u32[]{:S(2)}) async-start(s32[8,1,2]{2,1,0:T(1,128)} %bitcast.3), calls=%async_computation | async-start | bytes 8192 | tf_op jit(solution)/shard_map/all_to_all | solution.py:34
  34.0 4.3 %copy-start.2 = (bf16[384,3,512]{2,0,1:T(8,128)(2,1)S(1)}, bf16[384,3,512]{2,0,1:T(8,128)(2,1)}, u32[]{:S(2)}) copy-start(bf16[384,3,512]{2,0,1:T(8,128)(2,1)} %param.9) | copy-start | bytes 3538948
  34.0 104.6 %all-to-all-start.1 = ((f32[8,1,65536]{2,1,0:T(1,128)}), f32[8,1,65536]{2,1,0:T(1,128)S(1)}, u32[]{:S(2)}, u32[]{:S(2)}) async-start(f32[8,1,65536]{2,1,0:T(1,128)} %reshape.104), calls=%async_computation.1 | async-start | bytes 4194304 | tf_op jit(solution)/shard_map/all_to_all | solution.py:33
  38.2 287.7 %all-gather.11.cloned.1.call-start = ((), (), s32[]{:S(2)}) async-start(), calls=%async_computation.5 | async-start | bytes 3932160 | tf_op jit(solution)/shard_map/all_gather | solution.py:304
  138.6 1.3 copy-start
  251.6 125.6 %all-gather.7.cloned.1.call-start = ((), (), s32[]{:S(2)}) async-start(), calls=%async_computation.3 | async-start | bytes 3932160 | tf_op jit(solution)/shard_map/all_gather | solution.py:304
  377.3 4.6 %copy-start.3 = (bf16[768,768]{1,0:T(8,128)(2,1)S(1)}, bf16[768,768]{1,0:T(8,128)(2,1)}, u32[]{:S(2)}) copy-start(bf16[768,768]{1,0:T(8,128)(2,1)} %convolution_convert_fusion) | copy-start | bytes 3538948
Sparse Core Ops, SparseCore 0:
  10.6 115.2 all-gather.4
  127.5 89.3 all-gather.8
  251.7 61.8 all-gather.10
  315.1 62.1 all-gather.6
where the time goes:
time: 391 us; the launch traced here: 390 us
  Pallas kernels  201 us (51%)
  waiting for transfers between devices  71.3 us (18%)
  matrix products  42 us (11%)
  local copies, waits for them, and re-layouts  39.8 us (10%)
  between operations  13.9 us (4%)
  other arithmetic  12 us (3%)
  starting transfers between devices  9.6 us (2%)
    pallas_call x1, Pallas kernels, gather_rows(): pl.pallas_call(functools.partial(gather_kernel, chips, planes), out_shape...  93.7 us
    pallas_call x1, Pallas kernels, spread_columns(): pl.pallas_call(functools.partial(spread_kernel, count, planes), out_shape...  70.3 us
    all_gather x2, waiting for transfers between devices, body(): gathered.append(lax.all_gather(hidden, 'tp', axis=1, tiled=True))  45.8 us
    pallas_call x2, Pallas kernels, attend(): pl.pallas_call(functools.partial(attend_kernel, first, heads), out_shape=...  37.5 us
    dot_general x2, matrix products, body(): jnp.dot(features[c], weights, preferred_element_type=jnp.float32)  31.8 us
    all_gather x2, waiting for transfers between devices, body(): lax.all_gather(tokens[c * rows:(c + 1) * rows], 'tp', axis=1, tiled=True)  24.3 us
    unnamed x13, local copies, waits for them, and re-layouts  13.5 us
    dot_general x2, matrix products, body(): jnp.dot(part_heads, full_rows, preferred_element_type=jnp.float32)  10.2 us
  transfers between devices with their start and end apart: 6, of which 2 were waited for; matrix products, arithmetic and copies ran while one was open for 17% of the time, Pallas kernels for 47%

commit v1 on v0

--- a/solution.py
+++ b/solution.py
@@ -9,7 +9,6 @@
 
 HD = 64
 WINDOW_LENGTH = 128
-CHUNKS = 2
 
 
 def move_states(states, dest_slot):
@@ -55,7 +54,57 @@
     )
 
 
-def gather_kernel(chips, planes, w_ref, o_ref, out_ref, col_ref, send1, recv1, send2, recv2, sendz, recvz, local):
+def line_copies(planes, source_ref, all_ref, send, recv, local):
+    me = lax.axis_index("stream")
+    tp = lax.axis_index("tp")
+    wide = source_ref.shape[1]
+
+    def place(plane):
+        return all_ref.at[:, pl.ds(pl.multiple_of(plane * wide, wide), wide)]
+
+    out, back = [], []
+    for d in range(1, planes):
+        target = (me, (tp + d) % planes)
+        out.append(remote(source_ref, place(tp), send.at[d], recv.at[d], target))
+        source = (tp - d + planes) % planes
+        back.append(remote(source_ref, place(source), send.at[d], recv.at[d], target))
+    own = pltpu.make_async_copy(source_ref, place(tp), local)
+
+    def start():
+        for copy in out:
+            copy.start()
+        own.start()
+
+    def wait():
+        for copy in back:
+            copy.wait_recv()
+        for copy in out:
+            copy.wait_send()
+        own.wait()
+
+    return start, wait
+
+
+def gather_kernel(
+    chips,
+    planes,
+    rows,
+    w_ref,
+    o_ref,
+    t_ref,
+    out_ref,
+    col_ref,
+    feature_ref,
+    send1,
+    recv1,
+    send2,
+    recv2,
+    sendz,
+    recvz,
+    sendt,
+    recvt,
+    local,
+):
     me = lax.axis_index("stream")
     tp = lax.axis_index("tp")
     chip, core = me // 2, me % 2
@@ -74,6 +123,10 @@
     copy = remote(w_ref, out_ref.at[me], send2.at[0], recv2.at[0], sibling)
     copy.start()
     sends.append(copy)
+    start_line, wait_line = line_copies(
+        planes, t_ref.at[pl.ds(0, rows)], feature_ref, sendt, recvt, local.at[2]
+    )
+    start_line()
     hop = remote(o_ref, col_ref.at[tp], sendz, recvz.at[tp], (me, owner))
 
     @pl.when(jnp.logical_not(mine))
@@ -105,48 +158,55 @@
     def _():
         hop.wait_send()
 
+    wait_line()
     for copy in sends:
         copy.wait_send()
     own.wait()
     kept.wait()
 
 
-def gather_rows(weight, out_weight):
+def gather_rows(weight, out_weight, tokens, rows):
     count, planes = lax.axis_size("stream"), lax.axis_size("tp")
     chips = count // 2
     dma = pltpu.SemaphoreType.DMA
     anywhere = pl.BlockSpec(memory_space=pl.ANY)
     return pl.pallas_call(
-        functools.partial(gather_kernel, chips, planes),
+        functools.partial(gather_kernel, chips, planes, rows),
         out_shape=(
             jax.ShapeDtypeStruct((count,) + weight.shape, weight.dtype),
             jax.ShapeDtypeStruct((planes,) + out_weight.shape, out_weight.dtype),
+            jax.ShapeDtypeStruct((rows, planes * tokens.shape[1]), tokens.dtype),
         ),
-        in_specs=[anywhere, anywhere],
-        out_specs=(anywhere, anywhere),
-        scratch_shapes=[dma((chips,))] * 4 + [dma, dma((planes,)), dma((2,))],
+        in_specs=[anywhere] * 3,
+        out_specs=(anywhere,) * 3,
+        scratch_shapes=[dma((chips,))] * 4 + [dma] + [dma((planes,))] * 3 + [dma((3,))],
         compiler_params=pltpu.CompilerParams(collective_id=0, has_side_effects=True),
         cost_estimate=pl.CostEstimate(flops=0, bytes_accessed=200_000_000, transcendentals=0),
         name="gather_rows",
-    )(weight, out_weight)
-
-
-def spread_kernel(count, planes, col_ref, out_ref, sendx, recvx, sends, recvs, local):
+    )(weight, out_weight, tokens)
+
+
+def spread_kernel(
+    count, planes, col_ref, h_ref, out_ref, heads_ref, sendx, recvx, sends, recvs, sendh, recvh, local
+):
     me = lax.axis_index("stream")
     tp = lax.axis_index("tp")
     chips, per = count // 2, count // planes
     chip, core = me // 2, me % 2
     sibling = (chip * 2 + (1 - core), tp)
     peers = [(((chip + d) % chips) * 2 + core, tp) for d in range(1, chips)]
-    greet(peers + [sibling])
+    column = [(me, (tp + d) % planes) for d in range(1, planes)]
+    greet(peers + [sibling] + column)
     owner, place = me // per, me % per
+    start_line, wait_line = line_copies(planes, h_ref, heads_ref, sendh, recvh, local.at[1])
+    start_line()
     mine = owner == tp
 
     @pl.when(mine)
     def _():
         for d in range(1, chips):
             remote(col_ref, out_ref.at[place], sendx.at[d], recvx.at[place // 2], peers[d - 1]).start()
-        own = pltpu.make_async_copy(col_ref, out_ref.at[place], local)
+        own = pltpu.make_async_copy(col_ref, out_ref.at[place], local.at[0])
         own.start()
         own.wait()
 
@@ -171,21 +231,26 @@
         for d in range(1, chips):
             remote(col_ref, out_ref.at[place], sendx.at[d], recvx.at[place // 2], peers[d - 1]).wait_send()
 
-
-def spread_columns(columns):
+    wait_line()
+
+
+def spread_columns(columns, hidden):
     count, planes = lax.axis_size("stream"), lax.axis_size("tp")
     chips, per = count // 2, count // planes
     dma = pltpu.SemaphoreType.DMA
     return pl.pallas_call(
         functools.partial(spread_kernel, count, planes),
-        out_shape=jax.ShapeDtypeStruct((per,) + columns.shape, columns.dtype),
-        in_specs=[pl.BlockSpec(memory_space=pl.ANY)],
-        out_specs=pl.BlockSpec(memory_space=pl.ANY),
-        scratch_shapes=[dma((chips,)), dma((per // 2,)), dma((per // 2,)), dma((per // 2,)), dma],
+        out_shape=(
+            jax.ShapeDtypeStruct((per,) + columns.shape, columns.dtype),
+            jax.ShapeDtypeStruct((hidden.shape[0], planes * hidden.shape[1]), hidden.dtype),
+        ),
+        in_specs=[pl.BlockSpec(memory_space=pl.ANY)] * 2,
+        out_specs=(pl.BlockSpec(memory_space=pl.ANY),) * 2,
+        scratch_shapes=[dma((chips,))] + [dma((per // 2,))] * 3 + [dma((planes,))] * 2 + [dma((2,))],
         compiler_params=pltpu.CompilerParams(collective_id=1, has_side_effects=True),
         cost_estimate=pl.CostEstimate(flops=0, bytes_accessed=200_000_000, transcendentals=0),
         name="spread_columns",
-    )(columns)
+    )(columns, hidden)
 
 
 def halves(x):
@@ -286,24 +351,26 @@
 def body(tokens, qkv_weight, gate_weight, out_weight, log_decay, states, dest_slot, valid):
     streams, heads = states.shape[:2]
     width = heads * HD
-    chunks = CHUNKS if streams % CHUNKS == 0 else 1
-    part = streams // chunks
-    rows = part * WINDOW_LENGTH
-    features = [
-        lax.all_gather(tokens[c * rows : (c + 1) * rows], "tp", axis=1, tiled=True)
-        for c in range(chunks)
-    ]
+    lead, tail = streams // 6, streams // 3
+    middle = (streams - lead - tail) // 2
+    parts = [lead, middle, streams - lead - tail - middle, tail]
+    firsts = [sum(parts[:c]) for c in range(len(parts))]
+    features = [None]
+    for first, part in zip(firsts[1:], parts[1:]):
+        piece = tokens[first * WINDOW_LENGTH : (first + part) * WINDOW_LENGTH]
+        features.append(lax.all_gather(piece, "tp", axis=1, tiled=True))
     local = jnp.concatenate([qkv_weight.reshape(-1, 3 * width), gate_weight], axis=1)
     moved = move_states(states, dest_slot)
-    weights, columns = gather_rows(local, out_weight)
+    weights, columns, features[0] = gather_rows(local, out_weight, tokens, lead * WINDOW_LENGTH)
     weights = weights.reshape(-1, 4 * width)
     gathered, updated = [], None
-    for c in range(chunks):
+    for c, part in enumerate(parts):
         projected = jnp.dot(features[c], weights, preferred_element_type=jnp.float32)
-        hidden, updated = attend(projected, valid, log_decay, moved, c * part, part, updated)
-        gathered.append(lax.all_gather(hidden, "tp", axis=1, tiled=True))
-    columns, _ = lax.optimization_barrier((columns, hidden))
-    spread = spread_columns(columns)
+        hidden, updated = attend(projected, valid, log_decay, moved, firsts[c], part, updated)
+        if c + 1 < len(parts):
+            gathered.append(lax.all_gather(hidden, "tp", axis=1, tiled=True))
+    spread, heads_last = spread_columns(columns, hidden)
+    gathered.append(heads_last)
     per = spread.shape[0]
     full_rows = spread.reshape(per, -1, out_weight.shape[1]).transpose(1, 0, 2)
     full_rows = full_rows.reshape(full_rows.shape[0], -1)

time: 391 us -> 366 us (0.936)
  waiting for transfers between devices: 71.3 us -> 18.9 us
  Pallas kernels: 201 us -> 215 us
  matrix products: 42 us -> 53.7 us
    all_gather x2 -> x3, waiting for transfers between devices: 45.8 us -> 18.1 us  [body(): gathered.append(lax.all_gather(hidden, 'tp', axis=1, tiled=True))]
    all_gather x2 -> x3, waiting for transfers between devices: 24.3 us -> 0.06 us  [body(): features.append(lax.all_gather(piece, 'tp', axis=1, tiled=True))]
    dot_general x2 -> x4, matrix products: 31.8 us -> 41.8 us  [body(): jnp.dot(features[c], weights, preferred_element_type=jnp.float32)]
    pallas_call x1, Pallas kernels: 93.7 us -> 103 us  [gather_rows(): pl.pallas_call(functools.partial(gather_kernel, chips, planes, rows), out...]
    pallas_call x2 -> x4, Pallas kernels: 37.5 us -> 43 us  [attend(): pl.pallas_call(functools.partial(attend_kernel, first, heads), out_shape=...]
    dot_general x2 -> x4, matrix products: 10.2 us -> 11.9 us  [body(): jnp.dot(part_heads, full_rows, preferred_element_type=jnp.float32)]
    unnamed x13 -> x17, local copies, waits for them, and re-layouts: 13.5 us -> 13.6 us
  transfers between devices with their start and end apart: 6 -> 8, of which waited for: 2 -> 1; matrix products, arithmetic and copies ran while one was open for 17% -> 27% of each run, Pallas kernels for 47% -> 59%
where the time goes in v1:
time: 366 us; the launch traced here: 365 us
  Pallas kernels  215 us (59%)
  matrix products  53.7 us (15%)
  local copies, waits for them, and re-layouts  41 us (11%)
  waiting for transfers between devices  18.9 us (5%)
  between operations  14.3 us (4%)
  other arithmetic  12 us (3%)
  starting transfers between devices  9.78 us (3%)
    pallas_call x1, Pallas kernels, gather_rows(): pl.pallas_call(functools.partial(gather_kernel, chips, planes, rows), out...  103 us
    pallas_call x1, Pallas kernels, spread_columns(): pl.pallas_call(functools.partial(spread_kernel, count, planes), out_shape...  68.8 us
    pallas_call x4, Pallas kernels, attend(): pl.pallas_call(functools.partial(attend_kernel, first, heads), out_shape=...  43 us
    dot_general x4, matrix products, body(): jnp.dot(features[c], weights, preferred_element_type=jnp.float32)  41.8 us
    all_gather x3, waiting for transfers between devices, body(): gathered.append(lax.all_gather(hidden, 'tp', axis=1, tiled=True))  18.1 us
    unnamed x17, local copies, waits for them, and re-layouts  13.6 us
    dot_general x4, matrix products, body(): jnp.dot(part_heads, full_rows, preferred_element_type=jnp.float32)  11.9 us
  transfers between devices with their start and end apart: 8, of which 1 were waited for; matrix products, arithmetic and copies ran while one was open for 27% of the time, Pallas kernels for 59%

profile of v1, /device:TPU:0, one launch (start us, length us, event | category | flops | bytes accessed | tf_op | source)
XLA Modules:
  0.0 364.9 jit_solution(17149437765944350976)
XLA Ops:
  7.2 2.3 fusion.4
  10.4 2.2 slice.13
  14.2 5.2 %all-to-all-start = ((s32[8,1,2]{2,1,0:T(1,128)}), s32[8,1,2]{2,1,0:T(1,128)S(1)}, u32[]{:S(2)}, u32[]{:S(2)}) async-start(s32[8,1,2]{2,1,0:T(1,128)} %bitcast.2), calls=%async_computation | async-start | bytes 8192 | tf_op jit(solution)/shard_map/all_to_all | solution.py:33
  19.4 2.5 broadcast_in_dim.8
  21.8 6.3 %scatter_fusion = f32[16,8,64,64]{3,2,1,0:T(8,128)} fusion(f32[16,8,64,64]{3,2,1,0:T(8,128)} %broadcast_in_dim.8, s32[12]{0:T(128)S(1)} %compare_select_fusion.1, f32[12,8,64,64]{3,2,1,0:T(8,128)S(1)} %copy-done.1), kind=kCustom, calls=%fused_computation.1 | custom fusion | bytes 4718640 | tf_op jit(solution)/shard_map/scatter | solution.py:26
  28.1 7.2 %reshape.104 = f32[8,1,65536]{2,1,0:T(1,128)} reshape(f32[8,2,8,64,64]{4,3,2,1,0:T(8,128)} %bitcast.33) | data formatting | bytes 4194304
  35.3 4.4 %all-to-all-start.1 = ((f32[8,1,65536]{2,1,0:T(1,128)}), f32[8,1,65536]{2,1,0:T(1,128)S(1)}, u32[]{:S(2)}, u32[]{:S(2)}) async-start(f32[8,1,65536]{2,1,0:T(1,128)} %reshape.104), calls=%async_computation.1 | async-start | bytes 4194304 | tf_op jit(solution)/shard_map/all_to_all | solution.py:32
  39.7 1.4 copy.30
  41.1 1.6 copy.31
  42.7 2.4 pad_maximum_fusion.1.w_ref
  45.1 103.5 %gather_rows.1 = (bf16[8,384,2048]{2,1,0:T(8,128)(2,1)}, bf16[4,512,384]{2,1,0:T(8,128)(2,1)}, bf16[256,3072]{1,0:T(8,128)(2,1)}) custom-call(bf16[384,2048]{1,0:T(8,128)(2,1)} %pad_maximum_fusion.1.w_ref, bf16[512,384]{1,0:T(8,128)(2,1)} %o_ref.1, bf16[1536,768]{1,0:T(8,128)(2,1)} %t_ref.1), custom_call_target="tpu_custom_call" | custom-call | bytes 200000000 | tf_op jit(solution)/shard_map/gather_rows/pallas_call | solution.py:173
  148.5 9.9 %fusion.5.proj_ref = f32[256,2048]{1,0:T(8,128)} fusion(bf16[256,3072]{1,0:T(8,128)(2,1)} %get-tuple-element.15, bf16[3072,2048]{1,0:T(8,128)(2,1)} %bitcast.41), kind=kOutput, calls=%fused_computation.23 | convolution fusion | flops 3221225472 | bytes 16252928 | tf_op jit(solution)/shard_map/dot_general | solution.py:368
  159.7 1.3 copy-done
  161.5 7.2 %reduce.4 = f32[8,65536]{1,0:T(8,128)S(1)} reduce(f32[8,1,65536]{2,1,0:T(1,128)} %copy-done, f32[]{:T(128)} %broadcast.54), dimensions={1}, to_apply=%all_to_all.11.reduce_sub_computation | reduce | bytes 4194308 | tf_op jit(solution)/shard_map/all_to_all | solution.py:32
  168.8 3.6 reshape.105
  172.8 4.4 %scatter_fusion.1 = f32[13,8,64,64]{3,2,1,0:T(8,128)S(1)} fusion(f32[13,8,64,64]{3,2,1,0:T(8,128)S(1)} %broadcast_in_dim.6, s32[16]{0:T(128)S(1)} %fusion.1, f32[16,8,64,64]{3,2,1,0:T(8,128)} %bitcast.34), kind=kCustom, calls=%fused_computation.2 | custom fusion | bytes 6291520 | tf_op jit(solution)/shard_map/scatter | solution.py:37
  177.2 1.9 slice.16.moved_ref
  179.1 8.2 %attend.4 = (bf16[256,512]{1,0:T(8,128)(2,1)}, f32[12,8,64,64]{3,2,1,0:T(8,128)}) custom-call(s32[12]{0:T(128)} %valid_ref.7, f32[256,2048]{1,0:T(8,128)} %fusion.5.proj_ref, f32[8,1536]{1,0:T(8,128)} %decay_ref.7, f32[12,8,64,64]{3,2,1,0:T(8,128)} %slice.16.moved_ref), custom_call_target="tpu_custom_call" | custom-call | bytes 40000000 | tf_op jit(solution)/shard_map/attend/pallas_call | solution.py:330
  187.4 10.0 %convolution_bitcast_fusion.1.proj_ref = f32[384,2048]{1,0:T(8,128)} fusion(bf16[384,3072]{1,0:T(8,128)(2,1)} %all-gather.13.cloned.1.call-done, bf16[3072,2048]{1,0:T(8,128)(2,1)} %bitcast.42), kind=kOutput, calls=%fused_computation.4 | convolution fusion | flops 4831838208 | bytes 18087936 | tf_op jit(solution)/shard_map/dot_general | solution.py:368
  197.4 10.7 %attend.5 = (bf16[384,512]{1,0:T(8,128)(2,1)}, f32[12,8,64,64]{3,2,1,0:T(8,128)}) custom-call(s32[12]{0:T(128)} %valid_ref.7, f32[384,2048]{1,0:T(8,128)} %convolution_bitcast_fusion.1.proj_ref, f32[8,1536]{1,0:T(8,128)} %decay_ref.7, f32[12,8,64,64]{3,2,1,0:T(8,128)} %slice.16.moved_ref, ...), custom_call_target="tpu_custom_call", output_to_operand_aliasing={{1}: (4, {})} | custom-call | bytes 40000000 | tf_op jit(solution)/shard_map/attend/pallas_call | solution.py:330
  208.2 9.9 %convolution_bitcast_fusion.2.proj_ref = f32[384,2048]{1,0:T(8,128)} fusion(bf16[384,3072]{1,0:T(8,128)(2,1)} %all-gather.11.cloned.1.call-done, bf16[3072,2048]{1,0:T(8,128)(2,1)} %bitcast.43), kind=kOutput, calls=%fused_computation.5 | convolution fusion | flops 4831838208 | bytes 18087936 | tf_op jit(solution)/shard_map/dot_general | solution.py:368
  218.1 10.7 %attend.6 = (bf16[384,512]{1,0:T(8,128)(2,1)}, f32[12,8,64,64]{3,2,1,0:T(8,128)}) custom-call(s32[12]{0:T(128)} %valid_ref.7, f32[384,2048]{1,0:T(8,128)} %convolution_bitcast_fusion.2.proj_ref, f32[8,1536]{1,0:T(8,128)} %decay_ref.7, f32[12,8,64,64]{3,2,1,0:T(8,128)} %slice.16.moved_ref, ...), custom_call_target="tpu_custom_call", output_to_operand_aliasing={{1}: (4, {})} | custom-call | bytes 40000000 | tf_op jit(solution)/shard_map/attend/pallas_call | solution.py:330
  228.9 12.0 %convolution_bitcast_fusion.proj_ref = f32[512,2048]{1,0:T(8,128)} fusion(bf16[512,3072]{1,0:T(8,128)(2,1)} %all-gather.9.cloned.1.call-done, bf16[3072,2048]{1,0:T(8,128)(2,1)} %bitcast.44), kind=kOutput, calls=%fused_computation.3 | convolution fusion | flops 6442450944 | bytes 19922944 | tf_op jit(solution)/shard_map/dot_general | solution.py:368
  240.9 13.4 %attend.7 = (bf16[512,512]{1,0:T(8,128)(2,1)}, f32[12,8,64,64]{3,2,1,0:T(8,128)}) custom-call(s32[12]{0:T(128)} %valid_ref.7, f32[512,2048]{1,0:T(8,128)} %convolution_bitcast_fusion.proj_ref, f32[8,1536]{1,0:T(8,128)} %decay_ref.7, f32[12,8,64,64]{3,2,1,0:T(8,128)} %slice.16.moved_ref, ...), custom_call_target="tpu_custom_call", output_to_operand_aliasing={{1}: (4, {})} | custom-call | bytes 40000000 | tf_op jit(solution)/shard_map/attend/pallas_call | solution.py:330
  254.3 68.8 %spread_columns.1 = (bf16[2,4,512,384]{3,2,1,0:T(8,128)(2,1)}, bf16[512,2048]{1,0:T(8,128)(2,1)}) custom-call(bf16[4,512,384]{2,1,0:T(8,128)(2,1)} %get-tuple-element.18.col_ref, bf16[512,512]{1,0:T(8,128)(2,1)} %get-tuple-element.22.h_ref), custom_call_target="tpu_custom_call" | custom-call | bytes 200000000 | tf_op jit(solution)/shard_map/spread_columns/pallas_call | solution.py:241
  323.1 3.5 copy.36
  326.6 2.4 convolution_convert_fusion.3
  329.0 2.8 convolution_convert_fusion
  331.8 3.7 %convolution_convert_fusion.2 = bf16[384,768]{1,0:T(8,128)(2,1)} fusion(bf16[384,2048]{1,0:T(8,128)(2,1)} %all-gather.15.cloned.1.call-done, bf16[2048,768]{0,1:T(8,128)(2,1)S(1)} %bitcast.38), kind=kOutput, calls=%fused_computation.10 | convolution fusion | flops 1208254464 | bytes 5308416 | tf_op jit(solution)/shard_map/dot_general | solution.py:378
  335.5 18.0 %all-gather.17.cloned.1.call-done = bf16[384,2048]{1,0:T(8,128)(2,1)} async-done(((bf16[384,512]{1,0:T(8,128)(2,1)}), bf16[384,2048]{1,0:T(8,128)(2,1)}) %all-gather.17.cloned.1.call-update) | async-done | bytes 1572880 | tf_op jit(solution)/shard_map/all_gather | solution.py:371
  353.6 2.9 convolution_convert_fusion.1
  356.5 1.6 pad_maximum_fusion
  (43 shorter events, 4.8 us)
Async XLA Ops:
  7.2 5.5 %copy-start.6 = (s32[12]{0:T(128)S(1)}, s32[12]{0:T(128)}, u32[]{:S(2)}) copy-start(s32[12]{0:T(128)} %param.14) | copy-start | bytes 148
  7.2 180.2 %all-gather.13.cloned.1.call-start = ((), (), s32[]{:S(2)}) async-start(), calls=%async_computation.5 | async-start | bytes 2949120 | tf_op jit(solution)/shard_map/all_gather | solution.py:361
  9.6 198.6 %all-gather.11.cloned.1.call-start = ((), (), s32[]{:S(2)}) async-start(), calls=%async_computation.4 | async-start | bytes 2949120 | tf_op jit(solution)/shard_map/all_gather | solution.py:361
  10.3 11.5 %copy-start.1 = (f32[12,8,64,64]{3,2,1,0:T(8,128)S(1)}, f32[12,8,64,64]{3,2,1,0:T(8,128)}, u32[]{:S(2)}) copy-start(f32[12,8,64,64]{3,2,1,0:T(8,128)} %param.13) | copy-start | bytes 4718596
  10.4 218.5 %all-gather.9.cloned.1.call-start = ((), (), s32[]{:S(2)}) async-start(), calls=%async_computation.3 | async-start | bytes 3932160 | tf_op jit(solution)/shard_map/all_gather | solution.py:361
  14.2 21.1 %all-to-all-start = ((s32[8,1,2]{2,1,0:T(1,128)}), s32[8,1,2]{2,1,0:T(1,128)S(1)}, u32[]{:S(2)}, u32[]{:S(2)}) async-start(s32[8,1,2]{2,1,0:T(1,128)} %bitcast.2), calls=%async_computation | async-start | bytes 8192 | tf_op jit(solution)/shard_map/all_to_all | solution.py:33
  35.3 4.4 %copy-start.2 = (bf16[384,3,512]{2,0,1:T(8,128)(2,1)S(1)}, bf16[384,3,512]{2,0,1:T(8,128)(2,1)}, u32[]{:S(2)}) copy-start(bf16[384,3,512]{2,0,1:T(8,128)(2,1)} %param.9) | copy-start | bytes 3538948
  35.3 124.4 %all-to-all-start.1 = ((f32[8,1,65536]{2,1,0:T(1,128)}), f32[8,1,65536]{2,1,0:T(1,128)S(1)}, u32[]{:S(2)}, u32[]{:S(2)}) async-start(f32[8,1,65536]{2,1,0:T(1,128)} %reshape.104), calls=%async_computation.1 | async-start | bytes 4194304 | tf_op jit(solution)/shard_map/all_to_all | solution.py:32
  39.7 286.9 %all-gather.7.cloned.1.call-start = ((), (), s32[]{:S(2)}) async-start(), calls=%async_computation.2 | async-start | bytes 1310720 | tf_op jit(solution)/shard_map/all_gather | solution.py:371
  159.7 1.3 copy-start
  187.3 144.5 %all-gather.15.cloned.1.call-start = ((), (), s32[]{:S(2)}) async-start(), calls=%async_computation.6 | async-start | bytes 1966080 | tf_op jit(solution)/shard_map/all_gather | solution.py:371
  208.1 145.5 %all-gather.17.cloned.1.call-start = ((), (), s32[]{:S(2)}) async-start(), calls=%async_computation.7 | async-start | bytes 1966080 | tf_op jit(solution)/shard_map/all_gather | solution.py:371
  326.6 2.4 copy-start.5
  353.5 2.9 copy-start.3
  353.6 2.9 copy-start.4
Sparse Core Ops, SparseCore 0:
  9.7 75.8 all-gather.12
  87.2 64.2 all-gather.10
  153.0 62.4 all-gather.8
  217.0 26.6 all-gather.6
  245.0 70.7 all-gather.14
  317.3 36.2 all-gather.16

commit v2 on v1

--- a/solution.py
+++ b/solution.py
@@ -351,7 +351,7 @@
 def body(tokens, qkv_weight, gate_weight, out_weight, log_decay, states, dest_slot, valid):
     streams, heads = states.shape[:2]
     width = heads * HD
-    lead, tail = streams // 6, streams // 3
+    lead, tail = streams // 4, 5 * streams // 12
     middle = (streams - lead - tail) // 2
     parts = [lead, middle, streams - lead - tail - middle, tail]
     firsts = [sum(parts[:c]) for c in range(len(parts))]

time: 366 us -> 369 us (level)
  the two profiles are of different devices: /device:TPU:0 before, /device:TPU:8 now
where the time goes in v2:
time: 369 us; the launch traced here: 368 us
  Pallas kernels  237 us (64%)
  matrix products  56.2 us (15%)
  local copies, waits for them, and re-layouts  39.4 us (11%)
  between operations  14.3 us (4%)
  other arithmetic  12 us (3%)
  starting transfers between devices  8.07 us (2%)
    pallas_call x1, Pallas kernels, spread_columns(): pl.pallas_call(functools.partial(spread_kernel, count, planes), out_shape...  96.8 us
    pallas_call x1, Pallas kernels, gather_rows(): pl.pallas_call(functools.partial(gather_kernel, chips, planes, rows), out...  96.7 us
    dot_general x4, matrix products, body(): jnp.dot(features[c], weights, preferred_element_type=jnp.float32)  44.5 us
    pallas_call x4, Pallas kernels, attend(): pl.pallas_call(functools.partial(attend_kernel, first, heads), out_shape=...  43 us
    unnamed x17, local copies, waits for them, and re-layouts  13 us
    dot_general x4, matrix products, body(): jnp.dot(part_heads, full_rows, preferred_element_type=jnp.float32)  11.7 us
  transfers between devices with their start and end apart: 8, of which 0 were waited for; matrix products, arithmetic and copies ran while one was open for 27% of the time, Pallas kernels for 64%

profile of v2, /device:TPU:8, one launch (start us, length us, event | category | flops | bytes accessed | tf_op | source)
XLA Modules:
  0.0 367.9 jit_solution(12794712063636881737)
XLA Ops:
  7.2 2.1 fusion.4
  9.4 0.7 all-gather.11.cloned.1.call-update
  10.1 2.4 slice.13
  13.4 0.7 all_to_all.9
  14.0 3.7 %all-to-all-start = ((s32[8,1,2]{2,1,0:T(1,128)}), s32[8,1,2]{2,1,0:T(1,128)S(1)}, u32[]{:S(2)}, u32[]{:S(2)}) async-start(s32[8,1,2]{2,1,0:T(1,128)} %bitcast.2), calls=%async_computation | async-start | bytes 8192 | tf_op jit(solution)/shard_map/all_to_all | solution.py:33
  17.8 2.5 broadcast_in_dim.8
  20.2 6.3 %scatter_fusion = f32[16,8,64,64]{3,2,1,0:T(8,128)} fusion(f32[16,8,64,64]{3,2,1,0:T(8,128)} %broadcast_in_dim.8, s32[12]{0:T(128)S(1)} %compare_select_fusion.1, f32[12,8,64,64]{3,2,1,0:T(8,128)S(1)} %copy-done.1), kind=kCustom, calls=%fused_computation.1 | custom fusion | bytes 4718640 | tf_op jit(solution)/shard_map/scatter | solution.py:26
  26.5 7.3 %reshape.104 = f32[8,1,65536]{2,1,0:T(1,128)} reshape(f32[8,2,8,64,64]{4,3,2,1,0:T(8,128)} %bitcast.33) | data formatting | bytes 4194304
  33.8 0.7 copy.30
  35.2 4.1 %all-to-all-start.1 = ((f32[8,1,65536]{2,1,0:T(1,128)}), f32[8,1,65536]{2,1,0:T(1,128)S(1)}, u32[]{:S(2)}, u32[]{:S(2)}) async-start(f32[8,1,65536]{2,1,0:T(1,128)} %reshape.104), calls=%async_computation.1 | async-start | bytes 4194304 | tf_op jit(solution)/shard_map/all_to_all | solution.py:32
  39.4 2.4 pad_maximum_fusion.1.w_ref
  41.7 96.7 %gather_rows.1 = (bf16[8,384,2048]{2,1,0:T(8,128)(2,1)}, bf16[4,512,384]{2,1,0:T(8,128)(2,1)}, bf16[384,3072]{1,0:T(8,128)(2,1)}) custom-call(bf16[384,2048]{1,0:T(8,128)(2,1)} %pad_maximum_fusion.1.w_ref, bf16[512,384]{1,0:T(8,128)(2,1)} %o_ref.1, bf16[1536,768]{1,0:T(8,128)(2,1)} %t_ref.1), custom_call_target="tpu_custom_call" | custom-call | bytes 200000000 | tf_op jit(solution)/shard_map/gather_rows/pallas_call | solution.py:173
  138.5 10.8 %fusion.5.proj_ref = f32[384,2048]{1,0:T(8,128)} fusion(bf16[384,3072]{1,0:T(8,128)(2,1)} %get-tuple-element.15, bf16[3072,2048]{1,0:T(8,128)(2,1)} %bitcast.41), kind=kOutput, calls=%fused_computation.23 | convolution fusion | flops 4831838208 | bytes 18087936 | tf_op jit(solution)/shard_map/dot_general | solution.py:368
  150.6 1.3 copy-done
  152.4 7.2 %reduce.4 = f32[8,65536]{1,0:T(8,128)S(1)} reduce(f32[8,1,65536]{2,1,0:T(1,128)} %copy-done, f32[]{:T(128)} %broadcast.54), dimensions={1}, to_apply=%all_to_all.11.reduce_sub_computation | reduce | bytes 4194308 | tf_op jit(solution)/shard_map/all_to_all | solution.py:32
  159.6 3.6 reshape.105
  163.6 4.4 %scatter_fusion.1 = f32[13,8,64,64]{3,2,1,0:T(8,128)S(1)} fusion(f32[13,8,64,64]{3,2,1,0:T(8,128)S(1)} %broadcast_in_dim.6, s32[16]{0:T(128)S(1)} %fusion.1, f32[16,8,64,64]{3,2,1,0:T(8,128)} %bitcast.34), kind=kCustom, calls=%fused_computation.2 | custom fusion | bytes 6291520 | tf_op jit(solution)/shard_map/scatter | solution.py:37
  168.1 1.9 slice.16.moved_ref
  169.9 10.7 %attend.4 = (bf16[384,512]{1,0:T(8,128)(2,1)}, f32[12,8,64,64]{3,2,1,0:T(8,128)}) custom-call(s32[12]{0:T(128)} %valid_ref.7, f32[384,2048]{1,0:T(8,128)} %fusion.5.proj_ref, f32[8,1536]{1,0:T(8,128)} %decay_ref.7, f32[12,8,64,64]{3,2,1,0:T(8,128)} %slice.16.moved_ref), custom_call_target="tpu_custom_call" | custom-call | bytes 40000000 | tf_op jit(solution)/shard_map/attend/pallas_call | solution.py:330
  180.6 9.9 %convolution_bitcast_fusion.1.proj_ref = f32[256,2048]{1,0:T(8,128)} fusion(bf16[256,3072]{1,0:T(8,128)(2,1)} %all-gather.13.cloned.1.call-done, bf16[3072,2048]{1,0:T(8,128)(2,1)} %bitcast.42), kind=kOutput, calls=%fused_computation.4 | convolution fusion | flops 3221225472 | bytes 16252928 | tf_op jit(solution)/shard_map/dot_general | solution.py:368
  190.5 8.0 %attend.5 = (bf16[256,512]{1,0:T(8,128)(2,1)}, f32[12,8,64,64]{3,2,1,0:T(8,128)}) custom-call(s32[12]{0:T(128)} %valid_ref.7, f32[256,2048]{1,0:T(8,128)} %convolution_bitcast_fusion.1.proj_ref, f32[8,1536]{1,0:T(8,128)} %decay_ref.7, f32[12,8,64,64]{3,2,1,0:T(8,128)} %slice.16.moved_ref, ...), custom_call_target="tpu_custom_call", output_to_operand_aliasing={{1}: (4, {})} | custom-call | bytes 40000000 | tf_op jit(solution)/shard_map/attend/pallas_call | solution.py:330
  199.2 9.8 %convolution_bitcast_fusion.2.proj_ref = f32[256,2048]{1,0:T(8,128)} fusion(bf16[256,3072]{1,0:T(8,128)(2,1)} %all-gather.11.cloned.1.call-done, bf16[3072,2048]{1,0:T(8,128)(2,1)} %bitcast.43), kind=kOutput, calls=%fused_computation.5 | convolution fusion | flops 3221225472 | bytes 16252928 | tf_op jit(solution)/shard_map/dot_general | solution.py:368
  208.9 8.3 %attend.6 = (bf16[256,512]{1,0:T(8,128)(2,1)}, f32[12,8,64,64]{3,2,1,0:T(8,128)}) custom-call(s32[12]{0:T(128)} %valid_ref.7, f32[256,2048]{1,0:T(8,128)} %convolution_bitcast_fusion.2.proj_ref, f32[8,1536]{1,0:T(8,128)} %decay_ref.7, f32[12,8,64,64]{3,2,1,0:T(8,128)} %slice.16.moved_ref, ...), custom_call_target="tpu_custom_call", output_to_operand_aliasing={{1}: (4, {})} | custom-call | bytes 40000000 | tf_op jit(solution)/shard_map/attend/pallas_call | solution.py:330
  217.3 14.1 %convolution_bitcast_fusion.proj_ref = f32[640,2048]{1,0:T(8,128)} fusion(bf16[640,3072]{1,0:T(8,128)(2,1)} %all-gather.9.cloned.1.call-done, bf16[3072,2048]{1,0:T(8,128)(2,1)} %bitcast.44), kind=kOutput, calls=%fused_computation.3 | convolution fusion | flops 8053063680 | bytes 21757952 | tf_op jit(solution)/shard_map/dot_general | solution.py:368
  231.4 16.1 %attend.7 = (bf16[640,512]{1,0:T(8,128)(2,1)}, f32[12,8,64,64]{3,2,1,0:T(8,128)}) custom-call(s32[12]{0:T(128)} %valid_ref.7, f32[640,2048]{1,0:T(8,128)} %convolution_bitcast_fusion.proj_ref, f32[8,1536]{1,0:T(8,128)} %decay_ref.7, f32[12,8,64,64]{3,2,1,0:T(8,128)} %slice.16.moved_ref, ...), custom_call_target="tpu_custom_call", output_to_operand_aliasing={{1}: (4, {})} | custom-call | bytes 40000000 | tf_op jit(solution)/shard_map/attend/pallas_call | solution.py:330
  247.5 96.8 %spread_columns.1 = (bf16[2,4,512,384]{3,2,1,0:T(8,128)(2,1)}, bf16[640,2048]{1,0:T(8,128)(2,1)}) custom-call(bf16[4,512,384]{2,1,0:T(8,128)(2,1)} %get-tuple-element.18.col_ref, bf16[640,512]{1,0:T(8,128)(2,1)} %get-tuple-element.22.h_ref), custom_call_target="tpu_custom_call" | custom-call | bytes 200000000 | tf_op jit(solution)/shard_map/spread_columns/pallas_call | solution.py:241
  344.2 3.5 copy.36
  347.8 2.2 convolution_convert_fusion.3
  350.1 3.8 %convolution_convert_fusion.1 = bf16[384,768]{1,0:T(8,128)(2,1)} fusion(bf16[384,2048]{1,0:T(8,128)(2,1)} %all-gather.7.cloned.1.call-done, bf16[2048,768]{0,1:T(8,128)(2,1)S(1)} %bitcast.37), kind=kOutput, calls=%fused_computation.9 | convolution fusion | flops 1208254464 | bytes 5308416 | tf_op jit(solution)/shard_map/dot_general | solution.py:378
  353.9 3.3 convolution_convert_fusion
  357.1 2.4 convolution_convert_fusion.2
  359.5 1.6 pad_maximum_fusion
  (43 shorter events, 4.6 us)
Async XLA Ops:
  7.2 5.4 %copy-start.6 = (s32[12]{0:T(128)S(1)}, s32[12]{0:T(128)}, u32[]{:S(2)}) copy-start(s32[12]{0:T(128)} %param.14) | copy-start | bytes 148
  7.2 173.4 %all-gather.13.cloned.1.call-start = ((), (), s32[]{:S(2)}) async-start(), calls=%async_computation.5 | async-start | bytes 1966080 | tf_op jit(solution)/shard_map/all_gather | solution.py:361
  9.3 189.8 %all-gather.11.cloned.1.call-start = ((), (), s32[]{:S(2)}) async-start(), calls=%async_computation.4 | async-start | bytes 1966080 | tf_op jit(solution)/shard_map/all_gather | solution.py:361
  10.1 10.2 %copy-start.1 = (f32[12,8,64,64]{3,2,1,0:T(8,128)S(1)}, f32[12,8,64,64]{3,2,1,0:T(8,128)}, u32[]{:S(2)}) copy-start(f32[12,8,64,64]{3,2,1,0:T(8,128)} %param.13) | copy-start | bytes 4718596
  10.1 207.2 %all-gather.9.cloned.1.call-start = ((), (), s32[]{:S(2)}) async-start(), calls=%async_computation.3 | async-start | bytes 4915200 | tf_op jit(solution)/shard_map/all_gather | solution.py:361
  14.0 21.2 %all-to-all-start = ((s32[8,1,2]{2,1,0:T(1,128)}), s32[8,1,2]{2,1,0:T(1,128)S(1)}, u32[]{:S(2)}, u32[]{:S(2)}) async-start(s32[8,1,2]{2,1,0:T(1,128)} %bitcast.2), calls=%async_computation | async-start | bytes 8192 | tf_op jit(solution)/shard_map/all_to_all | solution.py:33
  26.5 7.3 %copy-start.2 = (bf16[384,3,512]{2,0,1:T(8,128)(2,1)S(1)}, bf16[384,3,512]{2,0,1:T(8,128)(2,1)}, u32[]{:S(2)}) copy-start(bf16[384,3,512]{2,0,1:T(8,128)(2,1)} %param.9) | copy-start | bytes 3538948
  35.2 115.3 %all-to-all-start.1 = ((f32[8,1,65536]{2,1,0:T(1,128)}), f32[8,1,65536]{2,1,0:T(1,128)S(1)}, u32[]{:S(2)}, u32[]{:S(2)}) async-start(f32[8,1,65536]{2,1,0:T(1,128)} %reshape.104), calls=%async_computation.1 | async-start | bytes 4194304 | tf_op jit(solution)/shard_map/all_to_all | solution.py:32
  39.4 308.4 %all-gather.15.cloned.1.call-start = ((), (), s32[]{:S(2)}) async-start(), calls=%async_computation.6 | async-start | bytes 1310720 | tf_op jit(solution)/shard_map/all_gather | solution.py:371
  150.5 1.3 copy-start
  198.5 151.6 %all-gather.7.cloned.1.call-start = ((), (), s32[]{:S(2)}) async-start(), calls=%async_computation.2 | async-start | bytes 1966080 | tf_op jit(solution)/shard_map/all_gather | solution.py:371
  199.1 158.1 %all-gather.17.cloned.1.call-start = ((), (), s32[]{:S(2)}) async-start(), calls=%async_computation.7 | async-start | bytes 1310720 | tf_op jit(solution)/shard_map/all_gather | solution.py:371
  350.1 3.8 %copy-start.5 = (bf16[640,2048]{1,0:T(8,128)(2,1)S(1)}, bf16[640,2048]{1,0:T(8,128)(2,1)}, u32[]{:S(2)}) copy-start(bf16[640,2048]{1,0:T(8,128)(2,1)} %get-tuple-element.26) | copy-start | bytes 7864324
  357.1 2.4 copy-start.3
  357.1 2.4 copy-start.4
Sparse Core Ops, SparseCore 0:
  9.6 37.2 all-gather.12
  48.4 72.2 all-gather.10
  122.3 84.8 all-gather.8
  208.6 29.1 all-gather.14
  239.2 71.4 all-gather.6
  312.1 36.0 all-gather.16
